TPU v7x, 128 devices: a whole 4x4x4 slice. The times are simulated.
128 devices in a mesh: row: 8 (over x, y_hi), col: 16 (over y_lo, z, core).
Axes of the slice: x: 4, y: 4 (y_hi: 2, y_lo: 2; y = y_hi * 2 + y_lo), z: 4, core: 2. Of those that a mesh axis runs over, the one named last changes fastest.
Arguments:
- front_trailing: float32 [16384, 16384], P('row', 'col'), may hold values from -6 to 6
- panel_columns: float32 [16384, 1024], P('row', 'col'), may hold values from -0.1875 to 0.1875
- panel_rows: float32 [1024, 16384], P('row', 'col'), may hold values from -6 to 6
- pivots: int32 [1024], replicated, may hold values from 0 to 1023, each once
- diag_inverse: float32 [1024, 1024], replicated, may hold values from -0.1875 to 0.1875
- test_matrix: float32 [16384, 512], P('col'), may hold values from -0.046875 to 0.046875
Outputs:
- schur: float32 [16384, 16384], P('row', 'col')
- off_samples: float32 [16384, 512], P(('row', 'col'))
- leaf_blocks: float32 [16384, 128], P(('row', 'col'))
- group_gram: float32 [8, 512, 512], P('row')
Inputs may be any that keep to these rules, and one draw needn't show every extreme that they name: pivots names each of 0 to 1023 once.
All inputs are finite; a program needn't handle non-finite values.
Results may differ from a plain program's by a relative error of at most 0.000084.
Values sent between devices are 32-bit elements; how exact they have to be, the bound alone decides.
A program may use at most 128 MiB of HBM per device.

v0:
```python
import jax
import jax.numpy as jnp
from jax import lax
from jax.sharding import PartitionSpec as P

LEAF = 128


def swapped(block, axis, apart):
    count = lax.axis_size(axis)
    route = []
    for low in range(count):
        high = low | 1 << apart
        if high != low and high < count:
            route += [(low, high), (high, low)]
    return lax.ppermute(block, axis, route)


def from_root(block, axis, source):
    block = jnp.where(lax.axis_index(axis) == source, block, jnp.zeros_like(block))
    return lax.psum(block, axis)


def product(left, right):
    return jnp.dot(left, right, precision=lax.Precision.HIGHEST, preferred_element_type=jnp.float32)


def inner_gram(samples_local):
    return lax.dot_general(
        samples_local,
        samples_local,
        (((0,), (0,)), ((), ())),
        precision=lax.Precision.HIGHEST,
        preferred_element_type=jnp.float32,
    )


def body(front_trailing, panel_columns, panel_rows, pivots, diag_inverse, test_matrix):
    row_count = lax.axis_size("row")
    col_count = lax.axis_size("col")
    row_index = lax.axis_index("row")
    col_index = lax.axis_index("col")
    height, width = front_trailing.shape
    upper_full = lax.all_gather(panel_rows, "row", axis=0, tiled=True)
    upper = jnp.take(upper_full, pivots, axis=0)
    lower = product(lax.all_gather(panel_columns, "col", axis=1, tiled=True), diag_inverse)
    update = product(lower, upper)
    schur = front_trailing - update
    global_rows = row_index * height + jnp.arange(height, dtype=jnp.int32)
    global_cols = col_index * width + jnp.arange(width, dtype=jnp.int32)
    same_leaf = global_rows[:, None] // LEAF == global_cols[None, :] // LEAF
    masked = jnp.where(same_leaf, jnp.zeros_like(schur), schur)
    per_device = height // col_count
    summed = lax.psum(product(masked, test_matrix), "col")
    own_samples = lax.dynamic_slice_in_dim(summed, col_index * per_device, per_device, 0)
    gram = inner_gram(summed)
    partner = swapped(gram, "row", 0)
    group_gram = ((gram + partner) / (2 * height))[None]
    ratio = col_count // row_count
    blocks_count = width // LEAF
    region_start = col_index % ratio * width
    region = lax.dynamic_slice_in_dim(schur, region_start, width, 0)
    candidates = jnp.diagonal(
        region.reshape(blocks_count, LEAF, blocks_count, LEAF), axis1=0, axis2=2
    )
    candidates = jnp.moveaxis(candidates, -1, 0)
    received = [from_root(candidates, "col", row_index * ratio + source) for source in range(ratio)]
    stacked = jnp.stack(received).reshape(ratio * blocks_count, LEAF, LEAF)
    first_row = col_index * per_device
    picked = lax.dynamic_slice_in_dim(stacked, first_row // LEAF, per_device // LEAF, 0)
    leaf_blocks = picked.reshape(per_device, LEAF)
    return (schur, own_samples, leaf_blocks, group_gram)


def solution(mesh):
    placed = (P("row", "col"), P("row", "col"), P("row", "col"), P(), P(), P("col", None))
    return jax.shard_map(
        body,
        mesh=mesh,
        in_specs=placed,
        out_specs=(
            P("row", "col"),
            P(("row", "col"), None),
            P(("row", "col"), None),
            P("row", None, None),
        ),
        check_vma=False,
    )
```

profile of v0, /device:TPU:0, one launch (start us, length us, event | category | flops | bytes accessed | tf_op | source)
XLA Modules:
  0.0 403.2 jit_solution(12109506079082405454)
XLA Ops:
  7.2 0.7 all-gather.5.cloned.1.call-update
  8.0 0.7 all-gather.3.cloned.1.call-update
  8.8 0.7 compare_and_fusion
  9.5 0.7 fusion.19
  10.2 74.2 %all-gather.5.cloned.1.call-done = f32[1024,1024]{1,0:T(8,128)} async-done(((f32[128,1024]{1,0:T(8,128)}), f32[1024,1024]{1,0:T(8,128)}) %all-gather.5.cloned.1.call-update) | async-done | bytes 4194320 | tf_op jit(solution)/shard_map/all_gather | solution.py:44
  84.4 8.5 %gather_fusion = f32[1024,1024]{1,0:T(8,128)} fusion(f32[1024,1024]{1,0:T(8,128)} %all-gather.5.cloned.1.call-done, s32[1024]{0:T(1024)S(1)} %fusion.19), kind=kCustom, calls=%fused_computation | custom fusion | bytes 8392704 | tf_op jit(solution)/shard_map/jit(_take)/gather | solution.py:45
  92.9 43.2 %all-gather.3.cloned.1.call-done = f32[2048,1024]{0,1:T(8,128)} async-done(((f32[2048,64]{0,1:T(8,128)}), f32[2048,1024]{0,1:T(8,128)}) %all-gather.3.cloned.1.call-update) | async-done | bytes 8388624 | tf_op jit(solution)/shard_map/all_gather | solution.py:46
  136.1 30.1 %fusion.22 = f32[2048,1024]{1,0:T(8,128)S(1)} fusion(f32[2048,1024]{0,1:T(8,128)} %all-gather.3.cloned.1.call-done, f32[1024,1024]{1,0:T(8,128)} %param.10), kind=kOutput, calls=%fused_computation.45 | convolution fusion | flops 25769803776 | bytes 20971520 | tf_op jit(solution)/shard_map/dot_general | solution.py:25
  166.2 29.4 %fusion.8 = f32[2048,1024]{1,0:T(8,128)S(1)} fusion(f32[2048,1024]{1,0:T(8,128)S(1)} %copy-done.3, f32[2048,1024]{1,0:T(8,128)S(1)} %fusion.22, f32[1024,1024]{1,0:T(8,128)S(1)} %copy-done.1, pred[1024]{0:T(1024)(128)(4,1)S(1)} %compare_and_fusion), kind=kOutput, calls=%fused_computation.12 | convolution fusion | flops 25772949504 | bytes 29361152 | tf_op jit(solution)/shard_map/dot_general | solution.py:25
  195.7 0.3 dynamic-slice_bitcast_fusion
  196.0 3.1 copy-done.2
  199.1 1.0 copy.12
  200.1 2.7 copy.14
  202.8 2.8 gather_fusion.1
  205.6 17.4 %fusion = f32[2048,512]{1,0:T(8,128)} fusion(f32[1024,512]{1,0:T(8,128)S(1)} %copy-done, f32[2048,1024]{1,0:T(8,128)} %copy-done.2, s32[1024]{0:T(1024)S(1)} %add_select_fusion.1, s32[2048]{0:T(1024)S(1)} %add_select_fusion), kind=kOutput, calls=%fused_computation.2 | convolution fusion | flops 12889096192 | bytes 14692352 | tf_op jit(solution)/shard_map/dot_general | solution.py:25
  222.9 1.1 select_bitcast_fusion.1
  224.0 134.5 %all-reduce.3.cloned.1.call-done = (f32[2048,512]{1,0:T(8,128)}, f32[1,8,128,128]{3,2,1,0:T(8,128)}, f32[1,8,128,128]{3,2,1,0:T(8,128)}) async-done(((f32[2048,512]{1,0:T(8,128)}, f32[1,8,128,128]{3,2,1,0:T(8,128)}, f32[1,8,128,128]{3,2,1,0:T(8,128)}), (f32[2048,512]{1,0:T(8,128)}, f32[1,8,128,128]{3,2,1,0:T(8,128)}, f32[1,8,128,128]{3,2,1,0:T(8,128)})) %all-reduce.3.cloned.1.call-update) | async-done | bytes 5242896 | tf_op jit(solution)/shard_map/psum | solution.py:54
  358.5 10.2 %fusion.23 = f32[512,512]{1,0:T(8,128)S(1)} fusion(f32[2048,512]{1,0:T(8,128)} %get-tuple-element.4), kind=kOutput, calls=%fused_computation.46 | convolution fusion | flops 6442450944 | bytes 5242880 | tf_op jit(solution)/shard_map/dot_general | solution.py:29
  368.7 2.8 collective-permute-start
  371.5 1.3 pad_maximum_fusion
  372.8 0.6 dynamic-slice_bitcast_fusion.1
  373.4 1.7 constant_dynamic-slice_fusion
  375.1 19.2 %collective-permute-done = f32[512,512]{1,0:T(8,128)} collective-permute-done((f32[512,512]{1,0:T(8,128)S(1)}, f32[512,512]{1,0:T(8,128)}, u32[]{:S(2)}, u32[]{:S(2)}) %collective-permute-start) | collective-permute-done | bytes 1048608 | tf_op jit(solution)/shard_map/ppermute | solution.py:16
  394.2 2.4 multiply_bitcast_fusion
  (14 shorter events, 0.2 us)
Async XLA Ops:
  7.2 198.4 %copy-start = (f32[1024,512]{1,0:T(8,128)S(1)}, f32[1024,512]{1,0:T(8,128)}, u32[]{:S(2)}) copy-start(f32[1024,512]{1,0:T(8,128)} %param.11) | copy-start | bytes 6291460
  7.2 77.2 %all-gather.5.cloned.1.call-start = ((), (), s32[]{:S(2)}) async-start(), calls=%async_computation.1 | async-start | bytes 4718592 | tf_op jit(solution)/shard_map/all_gather | solution.py:44
  7.9 128.2 %all-gather.3.cloned.1.call-start = ((), (), s32[]{:S(2)}) async-start(), calls=%async_computation | async-start | bytes 8912896 | tf_op jit(solution)/shard_map/all_gather | solution.py:46
  8.7 349.8 %all-reduce.3.cloned.1.call-start = ((), (), s32[]{:S(2)}) async-start(), calls=%async_computation.2 | async-start | bytes 10485760 | tf_op jit(solution)/shard_map/psum | solution.py:54
  136.1 30.1 %copy-start.1 = (f32[1024,1024]{1,0:T(8,128)S(1)}, f32[1024,1024]{1,0:T(8,128)}, u32[]{:S(2)}) copy-start(f32[1024,1024]{1,0:T(8,128)} %gather_fusion) | copy-start | bytes 12582916
  136.1 30.1 %copy-start.3 = (f32[2048,1024]{1,0:T(8,128)S(1)}, f32[2048,1024]{1,0:T(8,128)}, u32[]{:S(2)}) copy-start(f32[2048,1024]{1,0:T(8,128)} %param.6) | copy-start | bytes 25165828
  195.7 3.4 copy-start.2
  368.7 25.6 %collective-permute-start = (f32[512,512]{1,0:T(8,128)S(1)}, f32[512,512]{1,0:T(8,128)}, u32[]{:S(2)}, u32[]{:S(2)}) collective-permute-start(f32[512,512]{1,0:T(8,128)S(1)} %fusion.23), channel_id=1, source_target_pairs={{0,16},{16,0},{32,48},{48,32},{64,80},{80,64},{96,112},{112,96},{1... | collective-permute-start | bytes 3145736 | tf_op jit(solution)/shard_map/ppermute | solution.py:16
Sparse Core Ops, SparseCore 0:
  10.3 74.0 all-gather.4
  86.1 49.9 all-gather.2
  224.1 134.3 all-reduce.2
where the time goes:
time: 404 us; the launch traced here: 403 us
  waiting for transfers between devices  272 us (67%)
  matrix products  87 us (22%)
  local copies, waits for them, and re-layouts  20.7 us (5%)
  between operations  13.9 us (3%)
  other arithmetic  6.2 us (2%)
    psum x1, waiting for transfers between devices, body(): summed = lax.psum(product(masked, test_matrix), 'col')  134 us
    dot_general x3, matrix products, product(): jnp.dot(left, right, precision=lax.Precision.HIGHEST, preferred_element_t...  76.9 us
    all_gather x1, waiting for transfers between devices, body(): upper_full = lax.all_gather(panel_rows, 'row', axis=0, tiled=True)  74.2 us
    all_gather x1, waiting for transfers between devices, body(): lax.all_gather(panel_columns, 'col', axis=1, tiled=True)  43.2 us
    ppermute x1, waiting for transfers between devices, swapped(): return lax.ppermute(block, axis, route)  19.2 us
    dot_general x1, matrix products, inner_gram(): lax.dot_general(samples_local, samples_local, (((0,), (0,)), ((), ())), p...  10.2 us
    gather x1, local copies, waits for them, and re-layouts, body(): upper = jnp.take(upper_full, pivots, axis=0)  8.52 us
  transfers between devices with their start and end apart: 4, of which 4 were waited for; matrix products, arithmetic and copies ran while one was open for 3% of the time, Pallas kernels for 0%

commit v1 on v0

--- a/solution.py
+++ b/solution.py
@@ -41,7 +41,9 @@
     row_index = lax.axis_index("row")
     col_index = lax.axis_index("col")
     height, width = front_trailing.shape
-    upper_full = lax.all_gather(panel_rows, "row", axis=0, tiled=True)
+    upper_full = jnp.concatenate(
+        lax.all_to_all(jnp.stack([panel_rows] * lax.axis_size("row")), "row", 0, 0), axis=0
+    )
     upper = jnp.take(upper_full, pivots, axis=0)
     lower = product(lax.all_gather(panel_columns, "col", axis=1, tiled=True), diag_inverse)
     update = product(lower, upper)

time: 404 us -> 378 us (0.936)
  waiting for transfers between devices: 272 us -> 235 us
  starting transfers between devices: 2.91 us -> 10 us
    all_gather x1 -> x0, waiting for transfers between devices: 74.2 us -> none  [body(): upper_full = lax.all_gather(panel_rows, 'row', axis=0, tiled=True)]
    all_to_all x0 -> x1, waiting for transfers between devices: none -> 59.5 us  [body(): lax.all_to_all(jnp.stack([panel_rows] * lax.axis_size('row')), 'row', 0, 0)]
    all_gather x1, waiting for transfers between devices: 43.2 us -> 18.9 us  [body(): lax.all_gather(panel_columns, 'col', axis=1, tiled=True)]
    all_to_all x0 -> x1, starting transfers between devices: none -> 7.17 us  [body(): lax.all_to_all(jnp.stack([panel_rows] * lax.axis_size('row')), 'row', 0, 0)]
  transfers between devices with their start and end apart: 4 -> 4, of which waited for: 4 -> 4; matrix products, arithmetic and copies ran while one was open for 3% -> 4% of each run, Pallas kernels for 0% -> 0%
where the time goes in v1:
time: 378 us; the launch traced here: 377 us
  waiting for transfers between devices  235 us (62%)
  matrix products  88.9 us (24%)
  local copies, waits for them, and re-layouts  24.4 us (6%)
  between operations  14.2 us (4%)
  starting transfers between devices  10 us (3%)
  other arithmetic  4.83 us (1%)
    psum x1, waiting for transfers between devices, body(): summed = lax.psum(product(masked, test_matrix), 'col')  137 us
    dot_general x3, matrix products, product(): jnp.dot(left, right, precision=lax.Precision.HIGHEST, preferred_element_t...  78.6 us
    all_to_all x1, waiting for transfers between devices, body(): lax.all_to_all(jnp.stack([panel_rows] * lax.axis_size('row')), 'row', 0, 0)  59.5 us
    ppermute x1, waiting for transfers between devices, swapped(): return lax.ppermute(block, axis, route)  19.2 us
    all_gather x1, waiting for transfers between devices, body(): lax.all_gather(panel_columns, 'col', axis=1, tiled=True)  18.9 us
    dot_general x1, matrix products, inner_gram(): lax.dot_general(samples_local, samples_local, (((0,), (0,)), ((), ())), p...  10.2 us
    gather x1, local copies, waits for them, and re-layouts, body(): upper = jnp.take(upper_full, pivots, axis=0)  8.61 us
  transfers between devices with their start and end apart: 4, of which 4 were waited for; matrix products, arithmetic and copies ran while one was open for 4% of the time, Pallas kernels for 0%

profile of v1, /device:TPU:0, one launch (start us, length us, event | category | flops | bytes accessed | tf_op | source)
XLA Modules:
  0.0 377.1 jit_solution(5725426877560470006)
XLA Ops:
  7.2 0.0 all-gather.2.cloned.1.call-start
  7.2 0.7 all-gather.2.cloned.1.call-update
  7.9 3.6 stack.8
  11.5 7.2 %all-to-all-start = ((f32[8,128,1024]{2,1,0:T(8,128)}), f32[8,128,1024]{2,1,0:T(8,128)}, u32[]{:S(2)}, u32[]{:S(2)}) async-start(f32[8,128,1024]{2,1,0:T(8,128)} %stack.8), calls=%async_computation | async-start | bytes 8388608 | tf_op jit(solution)/shard_map/all_to_all | solution.py:45
  18.8 59.5 %all-to-all-done = f32[8,128,1024]{2,1,0:T(8,128)} async-done(((f32[8,128,1024]{2,1,0:T(8,128)}), f32[8,128,1024]{2,1,0:T(8,128)}, u32[]{:S(2)}, u32[]{:S(2)}) %all-to-all-start) | async-done | bytes 4194336 | tf_op jit(solution)/shard_map/all_to_all | solution.py:45
  78.3 8.6 %gather_fusion = f32[1024,1024]{1,0:T(8,128)} fusion(f32[1024,1024]{1,0:T(8,128)} %bitcast, s32[1024]{0:T(1024)S(1)} %fusion.19), kind=kCustom, calls=%fused_computation | custom fusion | bytes 8392704 | tf_op jit(solution)/shard_map/jit(_take)/gather | solution.py:47
  86.9 18.9 %all-gather.2.cloned.1.call-done = f32[2048,1024]{0,1:T(8,128)} async-done(((f32[2048,64]{0,1:T(8,128)}), f32[2048,1024]{0,1:T(8,128)}) %all-gather.2.cloned.1.call-update) | async-done | bytes 8388624 | tf_op jit(solution)/shard_map/all_gather | solution.py:48
  105.8 30.1 %fusion.22 = f32[2048,1024]{1,0:T(8,128)S(1)} fusion(f32[2048,1024]{0,1:T(8,128)} %all-gather.2.cloned.1.call-done, f32[1024,1024]{1,0:T(8,128)} %param.10), kind=kOutput, calls=%fused_computation.45 | convolution fusion | flops 25769803776 | bytes 20971520 | tf_op jit(solution)/shard_map/dot_general | solution.py:25
  135.9 31.4 %fusion.8 = f32[2048,1024]{1,0:T(8,128)S(1)} fusion(f32[2048,1024]{1,0:T(8,128)} %param.6, f32[2048,1024]{1,0:T(8,128)S(1)} %fusion.22, f32[1024,1024]{1,0:T(8,128)S(1)} %copy-done.1, pred[1024]{0:T(1024)(128)(4,1)S(1)} %compare_and_fusion), kind=kOutput, calls=%fused_computation.12 | convolution fusion | flops 25772949504 | bytes 29361152 | tf_op jit(solution)/shard_map/dot_general | solution.py:25
  167.3 0.3 dynamic-slice_bitcast_fusion
  167.7 3.1 copy-done.2
  170.7 1.0 copy.12
  171.7 2.7 copy.14
  174.4 2.8 gather_fusion.1
  177.2 17.1 %fusion = f32[2048,512]{1,0:T(8,128)} fusion(f32[1024,512]{1,0:T(8,128)S(1)} %copy-done, f32[2048,1024]{1,0:T(8,128)} %copy-done.2, s32[1024]{0:T(1024)S(1)} %add_select_fusion.1, s32[2048]{0:T(1024)S(1)} %add_select_fusion), kind=kOutput, calls=%fused_computation.2 | convolution fusion | flops 12889096192 | bytes 14692352 | tf_op jit(solution)/shard_map/dot_general | solution.py:25
  194.4 1.1 select_bitcast_fusion.1
  195.5 136.6 %all-reduce.3.cloned.1.call-done = (f32[2048,512]{1,0:T(8,128)}, f32[1,8,128,128]{3,2,1,0:T(8,128)}, f32[1,8,128,128]{3,2,1,0:T(8,128)}) async-done(((f32[2048,512]{1,0:T(8,128)}, f32[1,8,128,128]{3,2,1,0:T(8,128)}, f32[1,8,128,128]{3,2,1,0:T(8,128)}), (f32[2048,512]{1,0:T(8,128)}, f32[1,8,128,128]{3,2,1,0:T(8,128)}, f32[1,8,128,128]{3,2,1,0:T(8,128)})) %all-reduce.3.cloned.1.call-update) | async-done | bytes 5242896 | tf_op jit(solution)/shard_map/psum | solution.py:56
  332.0 10.2 %fusion.23 = f32[512,512]{1,0:T(8,128)S(1)} fusion(f32[2048,512]{1,0:T(8,128)} %get-tuple-element.4), kind=kOutput, calls=%fused_computation.46 | convolution fusion | flops 6442450944 | bytes 5242880 | tf_op jit(solution)/shard_map/dot_general | solution.py:29
  342.3 2.8 collective-permute-start
  345.1 1.3 pad_maximum_fusion
  346.4 0.6 dynamic-slice_bitcast_fusion.1
  347.0 1.7 constant_dynamic-slice_fusion
  348.7 19.2 %collective-permute-done = f32[512,512]{1,0:T(8,128)} collective-permute-done((f32[512,512]{1,0:T(8,128)S(1)}, f32[512,512]{1,0:T(8,128)}, u32[]{:S(2)}, u32[]{:S(2)}) %collective-permute-start) | collective-permute-done | bytes 1048608 | tf_op jit(solution)/shard_map/ppermute | solution.py:16
  367.9 2.4 multiply_bitcast_fusion
  (14 shorter events, 0.1 us)
Async XLA Ops:
  7.2 170.0 %copy-start = (f32[1024,512]{1,0:T(8,128)S(1)}, f32[1024,512]{1,0:T(8,128)}, u32[]{:S(2)}) copy-start(f32[1024,512]{1,0:T(8,128)} %param.11) | copy-start | bytes 6291460
  7.2 98.6 %all-gather.2.cloned.1.call-start = ((), (), s32[]{:S(2)}) async-start(), calls=%async_computation.1 | async-start | bytes 8912896 | tf_op jit(solution)/shard_map/all_gather | solution.py:48
  11.5 7.3 %copy-start.3 = (s32[1024]{0:T(1024)S(1)}, s32[1024]{0:T(1024)}, u32[]{:S(2)}) copy-start(s32[1024]{0:T(1024)} %param.9) | copy-start | bytes 12292
  11.5 66.8 %all-to-all-start = ((f32[8,128,1024]{2,1,0:T(8,128)}), f32[8,128,1024]{2,1,0:T(8,128)}, u32[]{:S(2)}, u32[]{:S(2)}) async-start(f32[8,128,1024]{2,1,0:T(8,128)} %stack.8), calls=%async_computation | async-start | bytes 8388608 | tf_op jit(solution)/shard_map/all_to_all | solution.py:45
  18.7 313.4 %all-reduce.3.cloned.1.call-start = ((), (), s32[]{:S(2)}) async-start(), calls=%async_computation.2 | async-start | bytes 10485760 | tf_op jit(solution)/shard_map/psum | solution.py:56
  105.8 30.1 %copy-start.1 = (f32[1024,1024]{1,0:T(8,128)S(1)}, f32[1024,1024]{1,0:T(8,128)}, u32[]{:S(2)}) copy-start(f32[1024,1024]{1,0:T(8,128)} %gather_fusion) | copy-start | bytes 12582916
  167.3 3.4 copy-start.2
  342.3 25.6 %collective-permute-start = (f32[512,512]{1,0:T(8,128)S(1)}, f32[512,512]{1,0:T(8,128)}, u32[]{:S(2)}, u32[]{:S(2)}) collective-permute-start(f32[512,512]{1,0:T(8,128)S(1)} %fusion.23), channel_id=1, source_target_pairs={{0,16},{16,0},{32,48},{48,32},{64,80},{80,64},{96,112},{112,96},{1... | collective-permute-start | bytes 3145736 | tf_op jit(solution)/shard_map/ppermute | solution.py:16
Sparse Core Ops, SparseCore 0:
  9.7 96.0 all-gather.1
  195.6 136.4 all-reduce.2
